TPU v7x, 256 devices: a whole 4x4x8 slice. The times are simulated.
256 devices in a mesh: row: 16 (over z, y_lo), col: 16 (over x, y_hi, core).
Axes of the slice: x: 4, y: 4 (y_hi: 2, y_lo: 2; y = y_hi * 2 + y_lo), z: 8, core: 2. Of those that a mesh axis runs over, the one named last changes fastest.
Arguments:
- kernels: bfloat16 [7, 12288, 12288], P(None, 'row', 'col'), may hold values from -0.02734375 to 0.02734375
- prestress: float32 [4, 12288, 512], P(None, 'row'), may hold values from -6 to 6
- rates_hist: bfloat16 [4, 12288, 512], P(None, 'col'), may hold values from -1 to 1
- gain: float32 [12288], P('row'), may hold values from 0.3 to 3
Outputs:
- rates: bfloat16 [4, 12288, 512], P(None, 'col', 'row')
- tractions: float32 [4, 12288, 512], P(None, 'row', 'col')
All inputs are finite; a program needn't handle non-finite values.
Results may differ from a plain program's by a relative error of at most 0.0018.
Values may be sent and summed in bfloat16 or wider, within the bound.
No kernel may reach another device: no remote copies, remote signals or barrier semaphores. Data moves between devices by JAX's collectives and lax.ppermute only.
A program may use at most 128 MiB of HBM per device.

v0:
```python
import jax
import jax.numpy as jnp
from jax import lax
from jax.sharding import Mesh
from jax.sharding import PartitionSpec as P

ROW = ("row_0", "row_1")


def in_blocks(array, dim, size):
    lengths = array.shape
    tiles = array.reshape(*lengths[:dim], size, lengths[dim] // size, *lengths[dim + 1 :])
    return jnp.moveaxis(tiles, dim, 0)


def summed_on_arrival(array, axis, dim):
    tiles = in_blocks(array, dim, lax.axis_size(axis))
    arrived = lax.all_to_all(tiles, axis, split_axis=0, concat_axis=0, tiled=True)
    return arrived.sum(axis=0)


def sent_to_all(array, axis):
    copies = jnp.broadcast_to(array, (lax.axis_size(axis), *array.shape))
    return lax.all_to_all(copies, axis, split_axis=0, concat_axis=0, tiled=True)


def joined_along(tiles, dim):
    tiles = jnp.moveaxis(tiles, 0, dim)
    lengths = tiles.shape
    return tiles.reshape(*lengths[:dim], lengths[dim] * lengths[dim + 1], *lengths[dim + 2 :])


def gather_directly(array, axis, dim):
    tiles = sent_to_all(array, axis)
    return joined_along(tiles, dim)


def from_root(array, axes, root):
    array = jnp.where(lax.axis_index(axes) == root, array, jnp.zeros_like(array))
    for axis in axes:
        array = lax.psum(array, axis)
    return array


def per_device(kernels, prestress, rates_hist, gain):
    total_scen = rates_hist.shape[2]
    col_count = lax.axis_size("col")
    row_count = lax.axis_size(ROW)
    share_cols = total_scen // col_count
    share_rows = total_scen // row_count
    ratio = row_count // col_count
    my_col = lax.axis_index("col")
    my_row = lax.axis_index(ROW)
    moments = prestress.shape[0]
    history = rates_hist.shape[0]
    stored = [rates_hist[position] for position in range(history)]
    rate_list = []
    traction_list = []
    for moment in range(1, moments + 1):
        partial_value = jnp.zeros((kernels.shape[1], total_scen), jnp.float32)
        for offset in range(1, moment + history):
            partial_value = partial_value + jnp.dot(
                kernels[offset - 1],
                stored[history - 1 + moment - offset],
                preferred_element_type=jnp.float32,
            )
        load_share = lax.dynamic_slice_in_dim(
            prestress[moment - 1], my_col * share_cols, share_cols, 1
        )
        traction = summed_on_arrival(partial_value, "col", 1) + load_share
        rate_share = jnp.tanh(gain[:, None] * traction).astype(jnp.bfloat16)
        row_rates = gather_directly(rate_share, "col", 1)
        traction_list.append(traction)
        pieces = from_root(row_rates, ROW, my_col * ratio + 0)
        stored.append(pieces)
        rate_list.append(lax.dynamic_slice_in_dim(pieces, my_row * share_rows, share_rows, 1))
    return (jnp.stack(rate_list), jnp.stack(traction_list))


def solution(mesh):
    finer = Mesh(mesh.devices.reshape(8, 2, mesh.shape["col"]), ("row_0", "row_1", "col"))
    return jax.shard_map(
        per_device,
        mesh=finer,
        in_specs=(P(None, ROW, "col"), P(None, ROW, None), P(None, "col", None), P(ROW)),
        out_specs=(P(None, "col", ROW), P(None, ROW, "col")),
        check_vma=False,
    )
```

profile of v0, /device:TPU:102, one launch (start us, length us, event | category | flops | bytes accessed | tf_op | source)
XLA Modules:
  0.0 725.7 jit_solution(3225623726486954066)
XLA Ops:
  17.3 7.4 %all-to-all-start = ((f32[16,768,32]{1,2,0:T(8,128)}), f32[16,768,32]{1,2,0:T(8,128)S(1)}, u32[]{:S(2)}, u32[]{:S(2)}) async-start(f32[16,768,32]{1,2,0:T(8,128)} %bitcast.9), calls=%async_computation | async-start | bytes 3145728 | tf_op jit(solution)/shard_map/all_to_all | solution.py:18
  24.7 5.1 fusion.115
  30.1 15.9 %all-to-all-done = f32[16,768,32]{1,2,0:T(8,128)S(1)} async-done(((f32[16,768,32]{1,2,0:T(8,128)}), f32[16,768,32]{1,2,0:T(8,128)S(1)}, u32[]{:S(2)}, u32[]{:S(2)}) %all-to-all-start) | async-done | bytes 1572896 | tf_op jit(solution)/shard_map/all_to_all | solution.py:18
  47.2 6.2 all-to-all-start.1
  53.4 12.8 %all-to-all-done.1 = bf16[16,768,32]{1,2,0:T(8,128)(2,1)S(1)} async-done(((bf16[16,768,32]{1,2,0:T(8,128)(2,1)}), bf16[16,768,32]{1,2,0:T(8,128)(2,1)S(1)}, u32[]{:S(2)}, u32[]{:S(2)}) %all-to-all-start.1) | async-done | bytes 786464 | tf_op jit(solution)/shard_map/all_to_all | solution.py:24
  67.3 73.4 %all-reduce.9.cloned.1.call-done = bf16[768,512]{0,1:T(8,128)(2,1)} async-done(((bf16[768,512]{0,1:T(8,128)(2,1)}), bf16[768,512]{0,1:T(8,128)(2,1)}) %all-reduce.9.cloned.1.call-update) | async-done | bytes 786448 | tf_op jit(solution)/shard_map/psum | solution.py:41
  150.9 37.7 %all-reduce.11.cloned.1.call-done = bf16[768,512]{0,1:T(8,128)(2,1)} async-done(((bf16[768,512]{0,1:T(8,128)(2,1)}), bf16[768,512]{0,1:T(8,128)(2,1)}) %all-reduce.11.cloned.1.call-update) | async-done | bytes 786448 | tf_op jit(solution)/shard_map/psum | solution.py:41
  195.2 7.0 all-to-all-start.2
  203.5 20.0 %all-to-all-done.2 = f32[16,768,32]{1,2,0:T(8,128)S(1)} async-done(((f32[16,768,32]{1,2,0:T(8,128)}), f32[16,768,32]{1,2,0:T(8,128)S(1)}, u32[]{:S(2)}, u32[]{:S(2)}) %all-to-all-start.2) | async-done | bytes 1572896 | tf_op jit(solution)/shard_map/all_to_all | solution.py:18
  223.7 19.2 %all_to_all.40 = bf16[16,768,32]{1,2,0:T(8,128)(2,1)S(1)} all-to-all(bf16[16,768,32]{1,2,0:T(8,128)(2,1)S(1)} %broadcast_in_dim.17), channel_id=1, replica_groups=mesh['row_0'=8,'row_1'=2,'col'=16] {'col'}, dimensions={0} | all-to-all | bytes 1572864 | tf_op jit(solution)/shard_map/all_to_all | solution.py:24
  247.4 69.1 %all-reduce.13.cloned.1.call-done = bf16[768,512]{0,1:T(8,128)(2,1)} async-done(((bf16[768,512]{0,1:T(8,128)(2,1)}), bf16[768,512]{0,1:T(8,128)(2,1)}) %all-reduce.13.cloned.1.call-update) | async-done | bytes 786448 | tf_op jit(solution)/shard_map/psum | solution.py:41
  326.5 37.9 %all-reduce.15.cloned.1.call-done = bf16[768,512]{0,1:T(8,128)(2,1)} async-done(((bf16[768,512]{0,1:T(8,128)(2,1)}), bf16[768,512]{0,1:T(8,128)(2,1)}) %all-reduce.15.cloned.1.call-update) | async-done | bytes 786448 | tf_op jit(solution)/shard_map/psum | solution.py:41
  366.8 4.6 fusion.5
  371.5 7.0 all-to-all-start.4
  379.8 20.0 %all-to-all-done.4 = f32[16,768,32]{1,2,0:T(8,128)S(1)} async-done(((f32[16,768,32]{1,2,0:T(8,128)}), f32[16,768,32]{1,2,0:T(8,128)S(1)}, u32[]{:S(2)}, u32[]{:S(2)}) %all-to-all-start.4) | async-done | bytes 1572896 | tf_op jit(solution)/shard_map/all_to_all | solution.py:18
  400.0 19.2 %all_to_all.41 = bf16[16,768,32]{1,2,0:T(8,128)(2,1)S(1)} all-to-all(bf16[16,768,32]{1,2,0:T(8,128)(2,1)S(1)} %broadcast_in_dim.18), channel_id=1, replica_groups=mesh['row_0'=8,'row_1'=2,'col'=16] {'col'}, dimensions={0} | all-to-all | bytes 1572864 | tf_op jit(solution)/shard_map/all_to_all | solution.py:24
  426.7 66.2 %all-reduce.17.cloned.1.call-done = bf16[768,512]{0,1:T(8,128)(2,1)} async-done(((bf16[768,512]{0,1:T(8,128)(2,1)}), bf16[768,512]{0,1:T(8,128)(2,1)}) %all-reduce.17.cloned.1.call-update) | async-done | bytes 786448 | tf_op jit(solution)/shard_map/psum | solution.py:41
  502.9 37.8 %all-reduce.19.cloned.1.call-done = bf16[768,512]{0,1:T(8,128)(2,1)} async-done(((bf16[768,512]{0,1:T(8,128)(2,1)}), bf16[768,512]{0,1:T(8,128)(2,1)}) %all-reduce.19.cloned.1.call-update) | async-done | bytes 786448 | tf_op jit(solution)/shard_map/psum | solution.py:41
  543.2 5.0 fusion.2
  548.2 7.0 all-to-all-start.6
  556.5 20.0 %all-to-all-done.6 = f32[16,768,32]{1,2,0:T(8,128)S(1)} async-done(((f32[16,768,32]{1,2,0:T(8,128)}), f32[16,768,32]{1,2,0:T(8,128)S(1)}, u32[]{:S(2)}, u32[]{:S(2)}) %all-to-all-start.6) | async-done | bytes 1572896 | tf_op jit(solution)/shard_map/all_to_all | solution.py:18
  576.7 18.9 %all_to_all.42 = bf16[16,768,32]{1,2,0:T(8,128)(2,1)S(1)} all-to-all(bf16[16,768,32]{1,2,0:T(8,128)(2,1)S(1)} %broadcast_in_dim.19), channel_id=1, replica_groups=mesh['row_0'=8,'row_1'=2,'col'=16] {'col'}, dimensions={0} | all-to-all | bytes 1572864 | tf_op jit(solution)/shard_map/all_to_all | solution.py:24
  597.5 71.9 %all-reduce.21.cloned.1.call-done = bf16[768,512]{0,1:T(8,128)(2,1)} async-done(((bf16[768,512]{0,1:T(8,128)(2,1)}), bf16[768,512]{0,1:T(8,128)(2,1)}) %all-reduce.21.cloned.1.call-update) | async-done | bytes 786448 | tf_op jit(solution)/shard_map/psum | solution.py:41
  671.9 45.5 %all-reduce.23.cloned.1.call-done = bf16[768,512]{0,1:T(8,128)(2,1)} async-done(((bf16[768,512]{0,1:T(8,128)(2,1)}), bf16[768,512]{0,1:T(8,128)(2,1)}) %all-reduce.23.cloned.1.call-update) | async-done | bytes 786448 | tf_op jit(solution)/shard_map/psum | solution.py:41
  (106 shorter events, 76.5 us)
Async XLA Ops:
  7.2 2.5 copy-start
  17.3 28.8 %all-to-all-start = ((f32[16,768,32]{1,2,0:T(8,128)}), f32[16,768,32]{1,2,0:T(8,128)S(1)}, u32[]{:S(2)}, u32[]{:S(2)}) async-start(f32[16,768,32]{1,2,0:T(8,128)} %bitcast.9), calls=%async_computation | async-start | bytes 3145728 | tf_op jit(solution)/shard_map/all_to_all | solution.py:18
  29.8 16.3 %copy-start.14 = (f32[768]{0:T(1024)S(1)}, f32[768]{0:T(1024)}, u32[]{:S(2)}) copy-start(f32[768]{0:T(1024)} %param.7) | copy-start | bytes 9220
  47.2 19.0 %all-to-all-start.1 = ((bf16[16,768,32]{1,2,0:T(8,128)(2,1)}), bf16[16,768,32]{1,2,0:T(8,128)(2,1)S(1)}, u32[]{:S(2)}, u32[]{:S(2)}) async-start(bf16[16,768,32]{1,2,0:T(8,128)(2,1)} %broadcast_in_dim.16), calls=%async_computation.1 | async-start | bytes 1572864 | tf_op jit(solution)/shard_map/all_to_all | solution.py:24
  53.4 87.3 %all-reduce.9.cloned.1.call-start = ((), (), s32[]{:S(2)}) async-start(), calls=%async_computation.8 | async-start | bytes 1572864 | tf_op jit(solution)/shard_map/psum | solution.py:41
  67.2 121.4 %all-reduce.11.cloned.1.call-start = ((), (), s32[]{:S(2)}) async-start(), calls=%async_computation.9 | async-start | bytes 1572864 | tf_op jit(solution)/shard_map/psum | solution.py:41
  140.7 3.7 copy-start.1
  195.2 28.3 %all-to-all-start.2 = ((f32[16,768,32]{1,2,0:T(8,128)}), f32[16,768,32]{1,2,0:T(8,128)S(1)}, u32[]{:S(2)}, u32[]{:S(2)}) async-start(f32[16,768,32]{1,2,0:T(8,128)} %bitcast.17), calls=%async_computation.2 | async-start | bytes 3145728 | tf_op jit(solution)/shard_map/all_to_all | solution.py:18
  202.2 114.3 %all-reduce.13.cloned.1.call-start = ((), (), s32[]{:S(2)}) async-start(), calls=%async_computation.10 | async-start | bytes 1572864 | tf_op jit(solution)/shard_map/psum | solution.py:41
  203.5 39.4 %copy-start.10 = (f32[1,768,32]{1,2,0:T(8,128)}, f32[1,768,32]{1,2,0:T(8,128)S(1)}, u32[]{:S(2)}) copy-start(f32[1,768,32]{1,2,0:T(8,128)S(1)} %copy.13) | copy-start | bytes 294916
  223.7 20.4 %copy-start.2 = (bf16[4,768,512]{2,1,0:T(8,128)(2,1)S(1)}, bf16[4,768,512]{2,1,0:T(8,128)(2,1)}, u32[]{:S(2)}) copy-start(bf16[4,768,512]{2,1,0:T(8,128)(2,1)} %param.6) | copy-start | bytes 9437188
  243.9 120.5 %all-reduce.15.cloned.1.call-start = ((), (), s32[]{:S(2)}) async-start(), calls=%async_computation.11 | async-start | bytes 1572864 | tf_op jit(solution)/shard_map/psum | solution.py:41
  319.8 3.4 copy-start.15
  371.5 28.3 %all-to-all-start.4 = ((f32[16,768,32]{1,2,0:T(8,128)}), f32[16,768,32]{1,2,0:T(8,128)S(1)}, u32[]{:S(2)}, u32[]{:S(2)}) async-start(f32[16,768,32]{1,2,0:T(8,128)} %bitcast.25), calls=%async_computation.4 | async-start | bytes 3145728 | tf_op jit(solution)/shard_map/all_to_all | solution.py:18
  378.4 114.5 %all-reduce.17.cloned.1.call-start = ((), (), s32[]{:S(2)}) async-start(), calls=%async_computation.12 | async-start | bytes 1572864 | tf_op jit(solution)/shard_map/psum | solution.py:41
  379.8 20.1 %copy-start.12 = (f32[1,768,32]{1,2,0:T(8,128)}, f32[1,768,32]{1,2,0:T(8,128)S(1)}, u32[]{:S(2)}) copy-start(f32[1,768,32]{1,2,0:T(8,128)S(1)} %copy.15) | copy-start | bytes 294916
  400.0 20.2 %copy-start.3 = (bf16[4,768,512]{2,1,0:T(8,128)(2,1)S(1)}, bf16[4,768,512]{2,1,0:T(8,128)(2,1)}, u32[]{:S(2)}) copy-start(bf16[4,768,512]{2,1,0:T(8,128)(2,1)} %param.6) | copy-start | bytes 9437188
  420.1 120.6 %all-reduce.19.cloned.1.call-start = ((), (), s32[]{:S(2)}) async-start(), calls=%async_computation.13 | async-start | bytes 1572864 | tf_op jit(solution)/shard_map/psum | solution.py:41
  492.9 3.4 copy-start.16
  496.4 3.4 copy-start.17
  548.2 28.3 %all-to-all-start.6 = ((f32[16,768,32]{1,2,0:T(8,128)}), f32[16,768,32]{1,2,0:T(8,128)S(1)}, u32[]{:S(2)}, u32[]{:S(2)}) async-start(f32[16,768,32]{1,2,0:T(8,128)} %bitcast.33), calls=%async_computation.6 | async-start | bytes 3145728 | tf_op jit(solution)/shard_map/all_to_all | solution.py:18
  555.2 114.2 %all-reduce.21.cloned.1.call-start = ((), (), s32[]{:S(2)}) async-start(), calls=%async_computation.14 | async-start | bytes 1572864 | tf_op jit(solution)/shard_map/psum | solution.py:41
  596.6 73.6 %copy-start.13 = (f32[1,768,32]{1,2,0:T(8,128)S(1)}, f32[1,768,32]{1,2,0:T(8,128)}, u32[]{:S(2)}) copy-start(f32[1,768,32]{1,2,0:T(8,128)} %copy-done.12) | copy-start | bytes 294916
  596.6 120.7 %all-reduce.23.cloned.1.call-start = ((), (), s32[]{:S(2)}) async-start(), calls=%async_computation.15 | async-start | bytes 1572864 | tf_op jit(solution)/shard_map/psum | solution.py:41
  (7 other events, 16.8 us)
Sparse Core Ops, SparseCore 0:
  67.3 73.2 all-reduce.8
  143.2 45.3 all-reduce.10
  244.0 72.4 all-reduce.12
  319.0 45.3 all-reduce.14
  420.3 72.6 all-reduce.16
  495.4 45.3 all-reduce.18
  596.8 72.6 all-reduce.20
  672.0 45.3 all-reduce.22
where the time goes:
time: 729 us; the launch traced here: 726 us
  waiting for transfers between devices  528 us (72%)
  matrix products  71.1 us (10%)
  blocking collectives  57.2 us (8%)
  starting transfers between devices  35 us (5%)
  between operations  14.4 us (2%)
  local copies, waits for them, and re-layouts  13.8 us (2%)
    psum x8, waiting for transfers between devices, from_root(): array = lax.psum(array, axis)  440 us
    all_to_all x4, waiting for transfers between devices, summed_on_arrival(): lax.all_to_all(tiles, axis, split_axis=0, concat_axis=0, tiled=True)  76 us
    dot_general x22, matrix products, per_device(): jnp.dot(kernels[offset - 1], stored[history - 1 + moment - offset], prefe...  71.1 us
    all_to_all x3, blocking collectives, sent_to_all(): return lax.all_to_all(copies, axis, split_axis=0, concat_axis=0, tiled=True)  57.2 us
    all_to_all x4, starting transfers between devices, summed_on_arrival(): lax.all_to_all(tiles, axis, split_axis=0, concat_axis=0, tiled=True)  28.3 us
  transfers between devices with their start and end apart: 13, of which 13 were waited for; matrix products, arithmetic and copies ran while one was open for 7% of the time, Pallas kernels for 0%

commit v1 on v0

v1 whole, which is shorter than its diff:
```python
import jax
import jax.numpy as jnp
from jax import lax
from jax.sharding import Mesh
from jax.sharding import PartitionSpec as P

AXES = ("z", "yl", "x", "yh", "k")
SIZES = (8, 2, 4, 2, 2)
ROW = ("z", "yl")
CHIP = ("x", "yh")
COL = ("x", "yh", "k")


def pairs_of(move):
    def number(place):
        total = 0
        for size, at in zip(SIZES, place):
            total = total * size + at
        return total

    found = []
    for z in range(8):
        for yl in range(2):
            for u in range(8):
                for k in range(2):
                    to_z, to_yl, to_u, to_k = move(z, yl, u, k)
                    source = (z, yl, u // 2, u % 2, k)
                    target = (to_z, to_yl, to_u // 2, to_u % 2, to_k)
                    found.append((number(source), number(target)))
    return found


def moved(array, move):
    return lax.ppermute(array, AXES, pairs_of(move))


def other_core(array):
    return moved(array, lambda z, yl, u, k: (z, yl, u, 1 - k))


def by_scenario(rates, kernel):
    return lax.dot_general(
        rates, kernel, (((1,), (1,)), ((), ())), preferred_element_type=jnp.float32
    )


def per_device(kernels, prestress, rates_hist, gain):
    moments, rows, scen = prestress.shape
    history = rates_hist.shape[0]
    share = scen // 16
    core = lax.axis_index("k")
    my_col = lax.axis_index(COL)

    load = lax.dynamic_slice_in_dim(prestress, my_col * share, share, 2)
    load = jnp.swapaxes(load, 1, 2)

    def two_tiles(kernel):
        theirs = other_core(kernel)
        first = jnp.where(core == 0, kernel, theirs)
        second = jnp.where(core == 0, theirs, kernel)
        return first, second

    def known(moment):
        total = 0.0
        for offset in range(moment, moment + history):
            total = total + lax.dot_general(
                rates_hist[history - 1 + moment - offset],
                kernels[offset - 1],
                (((0,), (1,)), ((), ())),
                preferred_element_type=jnp.float32,
            )
        total = total.reshape(8, 2, share, rows)
        mine = lax.dynamic_index_in_dim(total, core, 1, keepdims=False)
        theirs = lax.dynamic_index_in_dim(total, 1 - core, 1, keepdims=False)
        return mine + other_core(theirs)

    tiles = [two_tiles(kernels[position]) for position in range(moments - 1)]
    known_parts = [known(moment) for moment in range(1, moments + 1)]
    gathered = []
    traction_list = []
    crossed_list = []
    last_rates = None
    for moment in range(1, moments + 1):
        partial_value = known_parts[moment - 1]
        for back in range(1, moment):
            first, second = tiles[back - 1]
            one, two = gathered[moment - back - 1]
            extra = by_scenario(one, first) + by_scenario(two, second)
            partial_value = partial_value + extra.reshape(partial_value.shape)
        arrived = lax.all_to_all(partial_value, CHIP, 0, 0, tiled=True)
        traction = arrived.sum(axis=0) + load[moment - 1]
        traction_list.append(traction)
        rate = jnp.tanh(gain[None, :] * traction).astype(jnp.bfloat16)
        if moment < moments:
            crossed = moved(rate, lambda z, yl, u, k: (u, yl, z, k))
            crossed_list.append(crossed)
            copies = jnp.broadcast_to(crossed, (16, *crossed.shape))
            joined = lax.all_to_all(copies, ROW, 0, 0, tiled=True)
            joined = joined.reshape(8, 2, share, rows)
            gathered.append(
                (joined[:, 0].reshape(8 * share, rows), joined[:, 1].reshape(8 * share, rows))
            )
        else:
            last_rates = moved(rate, lambda z, yl, u, k: (u, k, z, yl))
    early = moved(jnp.stack(crossed_list), lambda z, yl, u, k: (z, k, u, yl))
    rates = jnp.concatenate([early, last_rates[None]], axis=0)
    tractions = jnp.stack(traction_list)
    return jnp.swapaxes(rates, 1, 2), jnp.swapaxes(tractions, 1, 2)


def solution(mesh):
    finer = Mesh(mesh.devices.reshape(SIZES), AXES)
    return jax.shard_map(
        per_device,
        mesh=finer,
        in_specs=(P(None, ROW, COL), P(None, ROW, None), P(None, COL, None), P(ROW)),
        out_specs=(P(None, COL, ROW), P(None, ROW, COL)),
        check_vma=False,
    )
```

time: 729 us -> 250 us (0.34)
  waiting for transfers between devices: 528 us -> 68.9 us
  blocking collectives: 57.2 us -> 0 us
  starting transfers between devices: 35 us -> 72 us
  between operations: 14.4 us -> 1.19 us
  other arithmetic: 5.74 us -> 16.6 us
  local copies, waits for them, and re-layouts: 13.8 us -> 23.8 us
    psum x8 -> x0, waiting for transfers between devices: 440 us -> none  [from_root(): array = lax.psum(array, axis)]
    all_to_all x3 -> x0, blocking collectives: 57.2 us -> none  [sent_to_all(): return lax.all_to_all(copies, axis, split_axis=0, concat_axis=0, tiled=True)]
    all_to_all x5 -> x7, waiting for transfers between devices: 88.8 us -> 44.7 us  [the longest x4 29.4 us: per_device(): arrived = lax.all_to_all(partial_value, CHIP, 0, 0, tiled=True)]
    ppermute x0 -> x12, waiting for transfers between devices: none -> 24.2 us  [moved(): return lax.ppermute(array, AXES, pairs_of(move))]
    ppermute x0 -> x12, starting transfers between devices: none -> 24 us  [moved(): return lax.ppermute(array, AXES, pairs_of(move))]
    all_to_all x5 -> x7, starting transfers between devices: 34.5 us -> 48 us  [the longest x4 32.6 us: per_device(): arrived = lax.all_to_all(partial_value, CHIP, 0, 0, tiled=True)]
    unnamed x40 -> x59, local copies, waits for them, and re-layouts: 0.63 us -> 8.57 us
    add x4 -> x5, other arithmetic: 0.05 us -> 7.69 us  [the longest x3 6.65 us: per_device(): partial_value = partial_value + extra.reshape(partial_value.shape)]
  transfers between devices with their start and end apart: 13 -> 19, of which waited for: 13 -> 12; matrix products, arithmetic and copies ran while one was open for 7% -> 31% of each run, Pallas kernels for 0% -> 0%
where the time goes in v1:
time: 250 us; the launch traced here: 248 us
  starting transfers between devices  72 us (29%)
  waiting for transfers between devices  68.9 us (28%)
  matrix products  65.4 us (26%)
  local copies, waits for them, and re-layouts  23.8 us (10%)
  other arithmetic  16.6 us (7%)
    dot_general x16, matrix products, known(): lax.dot_general(rates_hist[history - 1 + moment - offset], kernels[offset...  47.5 us
    all_to_all x4, starting transfers between devices, per_device(): arrived = lax.all_to_all(partial_value, CHIP, 0, 0, tiled=True)  32.6 us
    all_to_all x4, waiting for transfers between devices, per_device(): arrived = lax.all_to_all(partial_value, CHIP, 0, 0, tiled=True)  29.4 us
    ppermute x12, waiting for transfers between devices, moved(): return lax.ppermute(array, AXES, pairs_of(move))  24.2 us
    ppermute x12, starting transfers between devices, moved(): return lax.ppermute(array, AXES, pairs_of(move))  24 us
    dot_general x12, matrix products, by_scenario(): lax.dot_general(rates, kernel, (((1,), (1,)), ((), ())), preferred_elemen...  17.9 us
    all_to_all x3, starting transfers between devices, per_device(): joined = lax.all_to_all(copies, ROW, 0, 0, tiled=True)  15.5 us
    all_to_all x3, waiting for transfers between devices, per_device(): joined = lax.all_to_all(copies, ROW, 0, 0, tiled=True)  15.4 us
  transfers between devices with their start and end apart: 19, of which 12 were waited for; matrix products, arithmetic and copies ran while one was open for 31% of the time, Pallas kernels for 0%

profile of v1, /device:TPU:102, one launch (start us, length us, event | category | flops | bytes accessed | tf_op | source)
XLA Modules:
  0.0 247.9 jit_solution(14888706472869825247)
XLA Ops:
  16.4 7.4 %all-to-all-start = ((f32[8,32,768]{2,1,0:T(8,128)}), f32[8,32,768]{2,1,0:T(8,128)S(1)}, u32[]{:S(2)}, u32[]{:S(2)}) async-start(f32[8,32,768]{2,1,0:T(8,128)} %bitcast_add_fusion.3), calls=%async_computation | async-start | bytes 1572864 | tf_op jit(solution)/shard_map/all_to_all | solution.py:90
  23.8 3.9 %slice_bitcast_fusion.1 = (bf16[768,768]{1,0:T(8,128)(2,1)}, bf16[768,768]{1,0:T(8,128)(2,1)}, bf16[768,768]{1,0:T(8,128)(2,1)}) fusion(bf16[7,768,768]{2,1,0:T(8,128)(2,1)} %param.4), kind=kLoop, calls=%fused_computation.31 | loop fusion | bytes 7077888 | tf_op jit(solution)/shard_map/squeeze | solution.py:68
  30.0 5.8 %all-to-all-done = f32[8,32,768]{2,1,0:T(8,128)S(1)} async-done(((f32[8,32,768]{2,1,0:T(8,128)}), f32[8,32,768]{2,1,0:T(8,128)S(1)}, u32[]{:S(2)}, u32[]{:S(2)}) %all-to-all-start) | async-done | bytes 786464 | tf_op jit(solution)/shard_map/all_to_all | solution.py:90
  36.5 8.4 %collective-permute-start.1 = (bf16[32,768]{1,0:T(8,128)(2,1)S(1)}, bf16[32,768]{1,0:T(8,128)(2,1)S(1)}, u32[]{:S(2)}, u32[]{:S(2)}) collective-permute-start(bf16[32,768]{1,0:T(8,128)(2,1)S(1)} %fusion.88), channel_id=1, source_target_pairs={{0,0},{1,1},{2,32},{3,33},{4,64},{5,65},{6,96},{7,97},{8,128},{9,1... | collective-permute-start | bytes 147464 | tf_op jit(solution)/shard_map/ppermute | solution.py:34
  51.9 5.2 %all-to-all-start.1 = ((bf16[16,32,768]{2,1,0:T(8,128)(2,1)}), bf16[16,32,768]{2,1,0:T(8,128)(2,1)S(1)}, u32[]{:S(2)}, u32[]{:S(2)}) async-start(bf16[16,32,768]{2,1,0:T(8,128)(2,1)} %broadcast_in_dim.16), calls=%async_computation.1 | async-start | bytes 1572864 | tf_op jit(solution)/shard_map/all_to_all | solution.py:98
  67.9 7.2 %all-to-all-done.1 = bf16[16,32,768]{2,1,0:T(8,128)(2,1)S(1)} async-done(((bf16[16,32,768]{2,1,0:T(8,128)(2,1)}), bf16[16,32,768]{2,1,0:T(8,128)(2,1)S(1)}, u32[]{:S(2)}, u32[]{:S(2)}) %all-to-all-start.1) | async-done | bytes 786464 | tf_op jit(solution)/shard_map/all_to_all | solution.py:98
  81.3 9.7 %all-to-all-start.2 = ((f32[8,32,768]{2,1,0:T(8,128)}), f32[8,32,768]{2,1,0:T(8,128)}, u32[]{:S(2)}, u32[]{:S(2)}) async-start(f32[8,32,768]{2,1,0:T(8,128)} %fusion.32), calls=%async_computation.2 | async-start | bytes 1572864 | tf_op jit(solution)/shard_map/all_to_all | solution.py:90
  90.9 3.5 %fusion.6 = f32[512,768]{1,0:T(8,128)} fusion(bf16[7,768,768]{2,1,0:T(8,128)(2,1)} %param.4, bf16[4,768,512]{2,1,0:T(8,128)(2,1)} %param.6), kind=kOutput, calls=%fused_computation.16 | convolution fusion | flops 603979776 | bytes 3538944 | tf_op jit(solution)/shard_map/dot_general | solution.py:66
  94.5 8.0 %all-to-all-done.2 = f32[8,32,768]{2,1,0:T(8,128)} async-done(((f32[8,32,768]{2,1,0:T(8,128)}), f32[8,32,768]{2,1,0:T(8,128)}, u32[]{:S(2)}, u32[]{:S(2)}) %all-to-all-start.2) | async-done | bytes 786464 | tf_op jit(solution)/shard_map/all_to_all | solution.py:90
  105.2 5.1 %collective-permute-start.4 = (bf16[32,768]{1,0:T(8,128)(2,1)S(1)}, bf16[32,768]{1,0:T(8,128)(2,1)S(1)}, u32[]{:S(2)}, u32[]{:S(2)}) collective-permute-start(bf16[32,768]{1,0:T(8,128)(2,1)S(1)} %fusion.85), channel_id=1, source_target_pairs={{0,0},{1,1},{2,32},{3,33},{4,64},{5,65},{6,96},{7,97},{8,128},{9,1... | collective-permute-start | bytes 147464 | tf_op jit(solution)/shard_map/ppermute | solution.py:34
  113.7 5.2 %collective-permute-done.4 = bf16[32,768]{1,0:T(8,128)(2,1)S(1)} collective-permute-done((bf16[32,768]{1,0:T(8,128)(2,1)S(1)}, bf16[32,768]{1,0:T(8,128)(2,1)S(1)}, u32[]{:S(2)}, u32[]{:S(2)}) %collective-permute-start.4) | collective-permute-done | bytes 49184 | tf_op jit(solution)/shard_map/ppermute | solution.py:34
  120.6 5.1 %all-to-all-start.3 = ((bf16[16,32,768]{2,1,0:T(8,128)(2,1)}), bf16[16,32,768]{2,1,0:T(8,128)(2,1)}, u32[]{:S(2)}, u32[]{:S(2)}) async-start(bf16[16,32,768]{2,1,0:T(8,128)(2,1)} %broadcast_in_dim.17), calls=%async_computation.3 | async-start | bytes 1572864 | tf_op jit(solution)/shard_map/all_to_all | solution.py:98
  136.6 6.4 %all-to-all-done.3 = bf16[16,32,768]{2,1,0:T(8,128)(2,1)} async-done(((bf16[16,32,768]{2,1,0:T(8,128)(2,1)}), bf16[16,32,768]{2,1,0:T(8,128)(2,1)}, u32[]{:S(2)}, u32[]{:S(2)}) %all-to-all-start.3) | async-done | bytes 786464 | tf_op jit(solution)/shard_map/all_to_all | solution.py:98
  148.6 6.5 %all-to-all-start.4 = ((f32[8,32,768]{2,1,0:T(8,128)}), f32[8,32,768]{2,1,0:T(8,128)}, u32[]{:S(2)}, u32[]{:S(2)}) async-start(f32[8,32,768]{2,1,0:T(8,128)} %fusion.31), calls=%async_computation.4 | async-start | bytes 1572864 | tf_op jit(solution)/shard_map/all_to_all | solution.py:90
  155.0 3.5 %fusion.1 = f32[512,768]{1,0:T(8,128)} fusion(bf16[7,768,768]{2,1,0:T(8,128)(2,1)} %param.4, bf16[4,768,512]{2,1,0:T(8,128)(2,1)} %param.6), kind=kOutput, calls=%fused_computation.11 | convolution fusion | flops 603979776 | bytes 3538944 | tf_op jit(solution)/shard_map/dot_general | solution.py:66
  162.1 3.6 %all-to-all-done.4 = f32[8,32,768]{2,1,0:T(8,128)} async-done(((f32[8,32,768]{2,1,0:T(8,128)}), f32[8,32,768]{2,1,0:T(8,128)}, u32[]{:S(2)}, u32[]{:S(2)}) %all-to-all-start.4) | async-done | bytes 786464 | tf_op jit(solution)/shard_map/all_to_all | solution.py:90
  168.4 5.3 %collective-permute-start.7 = (bf16[32,768]{1,0:T(8,128)(2,1)S(1)}, bf16[32,768]{1,0:T(8,128)(2,1)S(1)}, u32[]{:S(2)}, u32[]{:S(2)}) collective-permute-start(bf16[32,768]{1,0:T(8,128)(2,1)S(1)} %fusion.82), channel_id=1, source_target_pairs={{0,0},{1,1},{2,32},{3,33},{4,64},{5,65},{6,96},{7,97},{8,128},{9,1... | collective-permute-start | bytes 147464 | tf_op jit(solution)/shard_map/ppermute | solution.py:34
  177.2 5.0 %collective-permute-done.7 = bf16[32,768]{1,0:T(8,128)(2,1)S(1)} collective-permute-done((bf16[32,768]{1,0:T(8,128)(2,1)S(1)}, bf16[32,768]{1,0:T(8,128)(2,1)S(1)}, u32[]{:S(2)}, u32[]{:S(2)}) %collective-permute-start.7) | collective-permute-done | bytes 49184 | tf_op jit(solution)/shard_map/ppermute | solution.py:34
  183.7 5.1 %all-to-all-start.5 = ((bf16[16,32,768]{2,1,0:T(8,128)(2,1)}), bf16[16,32,768]{2,1,0:T(8,128)(2,1)}, u32[]{:S(2)}, u32[]{:S(2)}) async-start(bf16[16,32,768]{2,1,0:T(8,128)(2,1)} %broadcast_in_dim.18), calls=%async_computation.5 | async-start | bytes 1572864 | tf_op jit(solution)/shard_map/all_to_all | solution.py:98
  188.9 3.8 %add_add_fusion = f32[512,768]{1,0:T(8,128)S(1)} fusion(f32[512,768]{1,0:T(8,128)} %fusion.1, f32[512,768]{1,0:T(8,128)} %fusion.9, f32[512,768]{1,0:T(8,128)} %fusion.4, bf16[7,768,768]{2,1,0:T(8,128)(2,1)} %param.4, bf16[4,768,512]{2,1,0:T(8,128)(2,1)} %param.6), kind=kOutput, calls=%fused_computation | convolution fusion | flops 605159424 | bytes 8257536 | tf_op jit(solution)/shard_map/dot_general | solution.py:66
  211.5 9.0 %all-to-all-start.6 = ((f32[8,32,768]{2,1,0:T(8,128)}), f32[8,32,768]{2,1,0:T(8,128)S(1)}, u32[]{:S(2)}, u32[]{:S(2)}) async-start(f32[8,32,768]{2,1,0:T(8,128)} %fusion.29), calls=%async_computation.6 | async-start | bytes 1572864 | tf_op jit(solution)/shard_map/all_to_all | solution.py:90
  221.3 12.0 %all-to-all-done.6 = f32[8,32,768]{2,1,0:T(8,128)S(1)} async-done(((f32[8,32,768]{2,1,0:T(8,128)}), f32[8,32,768]{2,1,0:T(8,128)S(1)}, u32[]{:S(2)}, u32[]{:S(2)}) %all-to-all-start.6) | async-done | bytes 786464 | tf_op jit(solution)/shard_map/all_to_all | solution.py:90
  233.4 4.4 %collective-permute-start.11 = (bf16[32,768]{1,0:T(8,128)(2,1)S(1)}, bf16[32,768]{1,0:T(8,128)(2,1)S(1)}, u32[]{:S(2)}, u32[]{:S(2)}) collective-permute-start(bf16[32,768]{1,0:T(8,128)(2,1)S(1)} %fusion.79), channel_id=1, source_target_pairs={{0,0},{1,16},{2,32},{3,48},{4,64},{5,80},{6,96},{7,112},{8,128},{9... | collective-permute-start | bytes 147464 | tf_op jit(solution)/shard_map/ppermute | solution.py:34
  238.6 8.6 %collective-permute-done.11 = bf16[32,768]{1,0:T(8,128)(2,1)S(1)} collective-permute-done((bf16[32,768]{1,0:T(8,128)(2,1)S(1)}, bf16[32,768]{1,0:T(8,128)(2,1)S(1)}, u32[]{:S(2)}, u32[]{:S(2)}) %collective-permute-start.11) | collective-permute-done | bytes 49184 | tf_op jit(solution)/shard_map/ppermute | solution.py:34
  (130 shorter events, 99.0 us)
Async XLA Ops:
  13.1 2.4 collective-permute-start
  16.4 19.4 %all-to-all-start = ((f32[8,32,768]{2,1,0:T(8,128)}), f32[8,32,768]{2,1,0:T(8,128)S(1)}, u32[]{:S(2)}, u32[]{:S(2)}) async-start(f32[8,32,768]{2,1,0:T(8,128)} %bitcast_add_fusion.3), calls=%async_computation | async-start | bytes 1572864 | tf_op jit(solution)/shard_map/all_to_all | solution.py:90
  27.7 38.4 %collective-permute-start.3 = (bf16[768,768]{1,0:T(8,128)(2,1)}, bf16[768,768]{1,0:T(8,128)(2,1)}, u32[]{:S(2)}, u32[]{:S(2)}) collective-permute-start(bf16[768,768]{1,0:T(8,128)(2,1)} %get-tuple-element.6), channel_id=1, source_target_pairs={{0,1},{1,0},{2,3},{3,2},{4,5},{5,4},{6,7},{7,6},{8,9},{9,8},{10,11... | collective-permute-start | bytes 3538952 | tf_op jit(solution)/shard_map/ppermute | solution.py:34
  36.5 13.8 %collective-permute-start.1 = (bf16[32,768]{1,0:T(8,128)(2,1)S(1)}, bf16[32,768]{1,0:T(8,128)(2,1)S(1)}, u32[]{:S(2)}, u32[]{:S(2)}) collective-permute-start(bf16[32,768]{1,0:T(8,128)(2,1)S(1)} %fusion.88), channel_id=1, source_target_pairs={{0,0},{1,1},{2,32},{3,33},{4,64},{5,65},{6,96},{7,97},{8,128},{9,1... | collective-permute-start | bytes 147464 | tf_op jit(solution)/shard_map/ppermute | solution.py:34
  51.9 23.2 %all-to-all-start.1 = ((bf16[16,32,768]{2,1,0:T(8,128)(2,1)}), bf16[16,32,768]{2,1,0:T(8,128)(2,1)S(1)}, u32[]{:S(2)}, u32[]{:S(2)}) async-start(bf16[16,32,768]{2,1,0:T(8,128)(2,1)} %broadcast_in_dim.16), calls=%async_computation.1 | async-start | bytes 1572864 | tf_op jit(solution)/shard_map/all_to_all | solution.py:98
  66.1 12.1 %collective-permute-start.2 = (f32[8,32,768]{2,1,0:T(8,128)}, f32[8,32,768]{2,1,0:T(8,128)}, u32[]{:S(2)}, u32[]{:S(2)}) collective-permute-start(f32[8,32,768]{2,1,0:T(8,128)} %dynamic-slice_bitcast_fusion.2), channel_id=1, source_target_pairs={{0,1},{1,0},{2,3},{3,2},{4,5},{5,4},{6,7},{7,6},{8,9},{9,8},{10,11... | collective-permute-start | bytes 2359304 | tf_op jit(solution)/shard_map/ppermute | solution.py:34
  77.2 54.5 %copy-start.12 = (bf16[8,1,32,768]{3,2,1,0:T(8,128)(2,1)}, bf16[8,1,32,768]{3,2,1,0:T(8,128)(2,1)S(1)}, u32[]{:S(2)}) copy-start(bf16[8,1,32,768]{3,2,1,0:T(8,128)(2,1)S(1)} %get-tuple-element.12) | copy-start | bytes 1179652
  81.3 21.2 %all-to-all-start.2 = ((f32[8,32,768]{2,1,0:T(8,128)}), f32[8,32,768]{2,1,0:T(8,128)}, u32[]{:S(2)}, u32[]{:S(2)}) async-start(f32[8,32,768]{2,1,0:T(8,128)} %fusion.32), calls=%async_computation.2 | async-start | bytes 1572864 | tf_op jit(solution)/shard_map/all_to_all | solution.py:90
  90.9 40.8 %collective-permute-start.6 = (bf16[768,768]{1,0:T(8,128)(2,1)}, bf16[768,768]{1,0:T(8,128)(2,1)}, u32[]{:S(2)}, u32[]{:S(2)}) collective-permute-start(bf16[768,768]{1,0:T(8,128)(2,1)} %get-tuple-element.4), channel_id=1, source_target_pairs={{0,1},{1,0},{2,3},{3,2},{4,5},{5,4},{6,7},{7,6},{8,9},{9,8},{10,11... | collective-permute-start | bytes 3538952 | tf_op jit(solution)/shard_map/ppermute | solution.py:34
  105.2 13.8 %collective-permute-start.4 = (bf16[32,768]{1,0:T(8,128)(2,1)S(1)}, bf16[32,768]{1,0:T(8,128)(2,1)S(1)}, u32[]{:S(2)}, u32[]{:S(2)}) collective-permute-start(bf16[32,768]{1,0:T(8,128)(2,1)S(1)} %fusion.85), channel_id=1, source_target_pairs={{0,0},{1,1},{2,32},{3,33},{4,64},{5,65},{6,96},{7,97},{8,128},{9,1... | collective-permute-start | bytes 147464 | tf_op jit(solution)/shard_map/ppermute | solution.py:34
  120.6 22.4 %all-to-all-start.3 = ((bf16[16,32,768]{2,1,0:T(8,128)(2,1)}), bf16[16,32,768]{2,1,0:T(8,128)(2,1)}, u32[]{:S(2)}, u32[]{:S(2)}) async-start(bf16[16,32,768]{2,1,0:T(8,128)(2,1)} %broadcast_in_dim.17), calls=%async_computation.3 | async-start | bytes 1572864 | tf_op jit(solution)/shard_map/all_to_all | solution.py:98
  131.7 13.6 %collective-permute-start.5 = (f32[8,32,768]{2,1,0:T(8,128)}, f32[8,32,768]{2,1,0:T(8,128)}, u32[]{:S(2)}, u32[]{:S(2)}) collective-permute-start(f32[8,32,768]{2,1,0:T(8,128)} %dynamic-slice_bitcast_fusion.1), channel_id=1, source_target_pairs={{0,1},{1,0},{2,3},{3,2},{4,5},{5,4},{6,7},{7,6},{8,9},{9,8},{10,11... | collective-permute-start | bytes 2359304 | tf_op jit(solution)/shard_map/ppermute | solution.py:34
  148.6 17.1 %all-to-all-start.4 = ((f32[8,32,768]{2,1,0:T(8,128)}), f32[8,32,768]{2,1,0:T(8,128)}, u32[]{:S(2)}, u32[]{:S(2)}) async-start(f32[8,32,768]{2,1,0:T(8,128)} %fusion.31), calls=%async_computation.4 | async-start | bytes 1572864 | tf_op jit(solution)/shard_map/all_to_all | solution.py:90
  155.0 38.6 %collective-permute-start.10 = (bf16[768,768]{1,0:T(8,128)(2,1)}, bf16[768,768]{1,0:T(8,128)(2,1)}, u32[]{:S(2)}, u32[]{:S(2)}) collective-permute-start(bf16[768,768]{1,0:T(8,128)(2,1)} %get-tuple-element.5), channel_id=1, source_target_pairs={{0,1},{1,0},{2,3},{3,2},{4,5},{5,4},{6,7},{7,6},{8,9},{9,8},{10,11... | collective-permute-start | bytes 3538952 | tf_op jit(solution)/shard_map/ppermute | solution.py:34
  168.4 13.8 %collective-permute-start.7 = (bf16[32,768]{1,0:T(8,128)(2,1)S(1)}, bf16[32,768]{1,0:T(8,128)(2,1)S(1)}, u32[]{:S(2)}, u32[]{:S(2)}) collective-permute-start(bf16[32,768]{1,0:T(8,128)(2,1)S(1)} %fusion.82), channel_id=1, source_target_pairs={{0,0},{1,1},{2,32},{3,33},{4,64},{5,65},{6,96},{7,97},{8,128},{9,1... | collective-permute-start | bytes 147464 | tf_op jit(solution)/shard_map/ppermute | solution.py:34
  183.7 22.0 %all-to-all-start.5 = ((bf16[16,32,768]{2,1,0:T(8,128)(2,1)}), bf16[16,32,768]{2,1,0:T(8,128)(2,1)}, u32[]{:S(2)}, u32[]{:S(2)}) async-start(bf16[16,32,768]{2,1,0:T(8,128)(2,1)} %broadcast_in_dim.18), calls=%async_computation.5 | async-start | bytes 1572864 | tf_op jit(solution)/shard_map/all_to_all | solution.py:98
  193.6 14.3 %collective-permute-start.9 = (f32[8,32,768]{2,1,0:T(8,128)}, f32[8,32,768]{2,1,0:T(8,128)}, u32[]{:S(2)}, u32[]{:S(2)}) collective-permute-start(f32[8,32,768]{2,1,0:T(8,128)} %dynamic-slice_bitcast_fusion), channel_id=1, source_target_pairs={{0,1},{1,0},{2,3},{3,2},{4,5},{5,4},{6,7},{7,6},{8,9},{9,8},{10,11... | collective-permute-start | bytes 2359304 | tf_op jit(solution)/shard_map/ppermute | solution.py:34
  211.5 9.0 %copy-start.27 = (bf16[32,768]{1,0:T(8,128)(2,1)S(1)}, bf16[32,768]{1,0:T(8,128)(2,1)}, u32[]{:S(2)}) copy-start(bf16[32,768]{1,0:T(8,128)(2,1)} %copy-done.26) | copy-start | bytes 147460
  211.5 21.8 %copy-start.19 = (f32[32,768]{1,0:T(8,128)S(1)}, f32[32,768]{1,0:T(8,128)}, u32[]{:S(2)}) copy-start(f32[32,768]{1,0:T(8,128)} %copy-done.18) | copy-start | bytes 294916
  211.5 21.8 %copy-start.20 = (f32[32,768]{1,0:T(8,128)S(1)}, f32[32,768]{1,0:T(8,128)}, u32[]{:S(2)}) copy-start(f32[32,768]{1,0:T(8,128)} %reduce_sum.45) | copy-start | bytes 294916
  211.5 21.8 %copy-start.21 = (f32[32,768]{1,0:T(8,128)S(1)}, f32[32,768]{1,0:T(8,128)}, u32[]{:S(2)}) copy-start(f32[32,768]{1,0:T(8,128)} %reduce_sum.46) | copy-start | bytes 294916
  211.5 21.7 %all-to-all-start.6 = ((f32[8,32,768]{2,1,0:T(8,128)}), f32[8,32,768]{2,1,0:T(8,128)S(1)}, u32[]{:S(2)}, u32[]{:S(2)}) async-start(f32[8,32,768]{2,1,0:T(8,128)} %fusion.29), calls=%async_computation.6 | async-start | bytes 1572864 | tf_op jit(solution)/shard_map/all_to_all | solution.py:90
  220.6 18.0 %collective-permute-start.8 = (bf16[3,32,768]{2,1,0:T(8,128)(2,1)S(1)}, bf16[3,32,768]{2,1,0:T(8,128)(2,1)S(1)}, u32[]{:S(2)}, u32[]{:S(2)}) collective-permute-start(bf16[3,32,768]{2,1,0:T(8,128)(2,1)S(1)} %pad_maximum_fusion), channel_id=1, source_target_pairs={{0,0},{1,16},{2,2},{3,18},{4,4},{5,20},{6,6},{7,22},{8,8},{9,24},{... | collective-permute-start | bytes 442376 | tf_op jit(solution)/shard_map/ppermute | solution.py:34
  233.4 13.8 %collective-permute-start.11 = (bf16[32,768]{1,0:T(8,128)(2,1)S(1)}, bf16[32,768]{1,0:T(8,128)(2,1)S(1)}, u32[]{:S(2)}, u32[]{:S(2)}) collective-permute-start(bf16[32,768]{1,0:T(8,128)(2,1)S(1)} %fusion.79), channel_id=1, source_target_pairs={{0,0},{1,16},{2,32},{3,48},{4,64},{5,80},{6,96},{7,112},{8,128},{9... | collective-permute-start | bytes 147464 | tf_op jit(solution)/shard_map/ppermute | solution.py:34
  (24 other events, 60.1 us)
